TPU v7x, 32 devices: a whole 2x2x4 slice. The times are simulated.
32 devices in a mesh: row: 8 (over z, y), col: 4 (over x, core).
Axes of the slice: x: 2, y: 2, z: 4, core: 2. Of those that a mesh axis runs over, the one named last changes fastest.
Arguments:
- trail_adjoint: float32 [4096, 4096], P('row', 'col'), may hold values from -6 to 6
- lower_new: float32 [4096, 256], P('row', 'col'), may hold values from -0.09375 to 0.09375
- upper_new: float32 [256, 4096], P('row', 'col'), may hold values from -0.09375 to 0.09375
- lower_old_top: float32 [256, 256], replicated, may hold values from -0.375 to 0.375
- lower_old: float32 [4096, 256], P('row', 'col'), may hold values from -0.09375 to 0.09375
- upper_old_left: float32 [256, 256], replicated, may hold values from -0.375 to 0.375
- upper_old: float32 [256, 4096], P('row', 'col'), may hold values from -0.09375 to 0.09375
- diag_lower_new: float32 [256, 256], replicated, as said below
- diag_upper_new: float32 [256, 256], replicated, as said below
- inverse_lower_new: float32 [256, 256], replicated, as said below
- inverse_upper_new: float32 [256, 256], replicated, as said below
- diag_lower_old: float32 [256, 256], replicated, as said below
- diag_upper_old: float32 [256, 256], replicated, as said below
- inverse_lower_old: float32 [256, 256], replicated, as said below
- inverse_upper_old: float32 [256, 256], replicated, as said below
Outputs:
- corner_old: float32 [256, 256], replicated
- strip_top: float32 [256, 256], replicated
- strip_bottom: float32 [4096, 256], P(('row', 'col'))
- band_left: float32 [256, 256], replicated
- band_right: float32 [256, 4096], P(None, 'col')
Inputs may be any that keep to these rules, and one draw needn't show every extreme that they name: `diag_lower_new`: unit lower triangular. `diag_upper_new`: upper triangular, diagonal from 1 to 2. `inverse_lower_new`: the inverse of diag_lower_new. `inverse_upper_new`: the inverse of diag_upper_new. `diag_lower_old`: unit lower triangular. `diag_upper_old`: upper triangular, diagonal from 1 to 2. `inverse_lower_old`: the inverse of diag_lower_old. `inverse_upper_old`: the inverse of diag_upper_old.
All inputs are finite; a program needn't handle non-finite values.
Results may differ from a plain program's by a relative error of at most 0.000075.
Values sent between devices are 32-bit elements; how exact they have to be, the bound alone decides.
A program may use at most 128 MiB of HBM per device.

v0:
```python
import jax
import jax.numpy as jnp
from jax import lax
from jax.sharding import PartitionSpec as P

precise = lax.Precision.HIGHEST


def times_trans(left, right):
    return lax.dot_general(left, right, (((1,), (1,)), ((), ())), precision=precise)


def trans_times(left, right):
    return lax.dot_general(left, right, (((0,), (0,)), ((), ())), precision=precise)


def diag_adjoint(lower_factor, upper_factor, lower_inverse, upper_inverse, lower_grad, upper_grad):
    inner = jnp.tril(trans_times(lower_factor, lower_grad), -1) + jnp.triu(
        times_trans(upper_grad, upper_factor)
    )
    return times_trans(trans_times(lower_inverse, inner), upper_inverse)


def upper_inner(terms):
    summed = lax.psum(terms, "col")
    return summed


def lower_inner(terms):
    summed = lax.psum(terms, "row")
    return summed


def body(
    trail_adjoint,
    lower_new,
    upper_new,
    lower_old_top,
    lower_old,
    upper_old_left,
    upper_old,
    diag_lower_new,
    diag_upper_new,
    inverse_lower_new,
    inverse_upper_new,
    diag_lower_old,
    diag_upper_old,
    inverse_lower_old,
    inverse_upper_old,
):
    width = inverse_lower_new.shape[0]
    lower_full_new, lower_full_old = (
        lax.all_gather(lower_new, "col", axis=1, tiled=True),
        lax.all_gather(lower_old, "col", axis=1, tiled=True),
    )
    upper_full_new, upper_full_old = (
        lax.all_gather(upper_new, "row", axis=0, tiled=True),
        lax.all_gather(upper_old, "row", axis=0, tiled=True),
    )
    lower_stack = jnp.concatenate((lower_full_new, lower_full_old), axis=1)
    upper_stack = jnp.concatenate((upper_full_new, upper_full_old), axis=0)
    portion = trail_adjoint.shape[0] // lax.axis_size("col")
    offset = lax.axis_index("col") * portion
    lower_adj = lax.psum(-times_trans(trail_adjoint, upper_stack), "col")
    lower_adj_new = lower_adj[:, :width]
    lower_adj_old = lower_adj[:, width:]
    strip_new = times_trans(lower_adj_new, inverse_upper_new)
    upper_adj = lax.psum(-trans_times(lower_stack, trail_adjoint), "row")
    band_new = trans_times(inverse_lower_new, upper_adj[:width])
    outer_new = upper_inner(
        (times_trans(band_new, upper_full_new), times_trans(band_new, upper_full_old))
    )
    inner_new = lower_inner(
        (trans_times(lower_full_new, strip_new), trans_times(lower_full_old, strip_new))
    )
    corner_new = diag_adjoint(
        diag_lower_new,
        diag_upper_new,
        inverse_lower_new,
        inverse_upper_new,
        -outer_new[0],
        -inner_new[0],
    )
    strip_top = times_trans(
        -(times_trans(corner_new, upper_old_left) + outer_new[1]), inverse_upper_old
    )
    strip_bottom = times_trans(
        lower_adj_old - times_trans(strip_new, upper_old_left), inverse_upper_old
    )
    band_left = trans_times(
        inverse_lower_old, -(trans_times(lower_old_top, corner_new) + inner_new[1])
    )
    band_right = trans_times(
        inverse_lower_old, upper_adj[width:] - trans_times(lower_old_top, band_new)
    )
    outer_old = upper_inner(times_trans(band_right, upper_full_old))
    inner_old = lower_inner(trans_times(lower_full_old, strip_bottom))
    lower_grad = -(times_trans(band_left, upper_old_left) + outer_old)
    upper_grad = -(trans_times(lower_old_top, strip_top) + inner_old)
    corner_old = diag_adjoint(
        diag_lower_old, diag_upper_old, inverse_lower_old, inverse_upper_old, lower_grad, upper_grad
    )
    strip_bottom = lax.dynamic_slice_in_dim(strip_bottom, offset, portion, 0)
    return (corner_old, strip_top, strip_bottom, band_left, band_right)


def solution(mesh):
    return jax.shard_map(
        body,
        mesh=mesh,
        in_specs=(
            P("row", "col"),
            P("row", "col"),
            P("row", "col"),
            P(),
            P("row", "col"),
            P(),
            P("row", "col"),
            P(),
            P(),
            P(),
            P(),
            P(),
            P(),
            P(),
            P(),
        ),
        out_specs=(P(), P(), P(("row", "col"), None), P(), P(None, "col")),
        check_vma=False,
    )
```

profile of v0, /device:TPU:0, one launch (start us, length us, event | category | flops | bytes accessed | tf_op | source)
XLA Modules:
  0.0 336.3 jit_solution(6877117094611444565)
XLA Ops:
  7.2 0.0 copy-start
  7.2 0.0 all-gather.3.cloned.1.call-start
  7.2 0.7 all-gather.3.cloned.1.call-update
  7.9 0.0 all-gather.5.cloned.1.call-start
  8.0 0.7 all-gather.5.cloned.1.call-update
  8.7 0.0 all-reduce.6.cloned.1.call-start
  8.7 8.9 %all_gather.13 = f32[512,256]{0,1:T(8,128)S(1)} all-gather(f32[512,64]{0,1:T(8,128)} %param.19), channel_id=1, replica_groups=mesh['row'=8,'col'=4] {'col'}, dimensions={1}, use_global_device_ids=true | all-gather | bytes 655360 | tf_op jit(solution)/shard_map/all_gather | solution.py:54
  17.6 35.6 %all-gather.3.cloned.1.call-done = f32[256,1024]{1,0:T(8,128)} async-done(((f32[32,1024]{1,0:T(8,128)}), f32[256,1024]{1,0:T(8,128)}) %all-gather.3.cloned.1.call-update) | async-done | bytes 1048592 | tf_op jit(solution)/shard_map/all_gather | solution.py:57
  53.1 41.1 %all-gather.5.cloned.1.call-done = f32[256,1024]{1,0:T(8,128)} async-done(((f32[32,1024]{1,0:T(8,128)}), f32[256,1024]{1,0:T(8,128)}) %all-gather.5.cloned.1.call-update) | async-done | bytes 1048592 | tf_op jit(solution)/shard_map/all_gather | solution.py:58
  94.3 0.0 copy-done
  94.3 6.0 %fusion.7 = f32[512,512]{0,1:T(8,128)} fusion(f32[512,1024]{1,0:T(8,128)S(1)} %copy-done, f32[256,1024]{1,0:T(8,128)} %all-gather.5.cloned.1.call-done, f32[256,1024]{1,0:T(8,128)} %all-gather.3.cloned.1.call-done), kind=kOutput, calls=%fused_computation.6 | convolution fusion | flops 3222011904 | bytes 5242880 | tf_op jit(solution)/shard_map/dot_general | solution.py:10
  100.3 0.0 all-reduce.6.cloned.1.call-update
  100.4 0.0 all-reduce.8.cloned.1.call-start
  100.4 7.8 %all_gather.12 = f32[512,256]{0,1:T(8,128)S(1)} all-gather(f32[512,64]{0,1:T(8,128)S(1)} %copy-done.22), channel_id=1, replica_groups=mesh['row'=8,'col'=4] {'col'}, dimensions={1}, use_global_device_ids=true | all-gather | bytes 655360 | tf_op jit(solution)/shard_map/all_gather | solution.py:53
  108.2 4.9 %convolution_negate_fusion = f32[512,1024]{1,0:T(8,128)} fusion(f32[512,1024]{1,0:T(8,128)S(1)} %copy-done, f32[512,256]{0,1:T(8,128)S(1)} %all_gather.13, f32[512,256]{0,1:T(8,128)S(1)} %all_gather.12), kind=kOutput, calls=%fused_computation.4 | convolution fusion | flops 3222011904 | bytes 5242880 | tf_op jit(solution)/shard_map/dot_general | solution.py:14
  113.2 22.4 %all-reduce.6.cloned.1.call-done = f32[512,512]{0,1:T(8,128)} async-done(((f32[512,512]{0,1:T(8,128)}), f32[512,512]{0,1:T(8,128)}) %all-reduce.6.cloned.1.call-update) | async-done | bytes 1048592 | tf_op jit(solution)/shard_map/psum | solution.py:64
  135.5 2.2 fusion.26
  137.7 0.0 copy-start.5
  137.7 1.7 convolution_bitcast_fusion.4
  139.5 1.7 convolution_bitcast_fusion.6
  141.2 0.7 convolution_subtract_fusion
  141.9 1.0 fusion.40
  142.9 0.0 copy-start.3
  142.9 0.8 copy-done.3
  143.7 1.7 convolution_bitcast_fusion.1
  145.4 0.0 all-reduce.8.cloned.1.call-update
  145.4 0.3 all-reduce.10.cloned.1.call-start
  145.7 123.1 %all-reduce.8.cloned.1.call-done = (f32[512,1024]{1,0:T(8,128)}, f32[256,256]{0,1:T(8,128)}, f32[256,256]{0,1:T(8,128)}, f32[256,256]{0,1:T(8,128)}) async-done(((f32[512,1024]{1,0:T(8,128)}, f32[256,256]{0,1:T(8,128)}, f32[256,256]{0,1:T(8,128)}, f32[256,256]{0,1:T(8,128)}), (f32[512,1024]{1,0:T(8,128)}, f32[256,256]{0,1:T(8,128)}, f32[256,256]{0,1:T(8,128)}, ...) | async-done | bytes 2883600 | tf_op jit(solution)/shard_map/psum | solution.py:68
  268.8 3.2 fusion.21
  272.0 0.0 copy-done.9
  272.0 0.0 copy-done.11
  272.0 0.0 copy-start.4
  272.0 1.1 fusion.10
  273.2 1.8 fusion.36
  275.0 0.0 copy-done.2
  275.0 2.5 fusion.32
  277.5 0.0 copy-done.1
  277.5 2.5 fusion.38
  280.0 2.5 fusion.37
  282.6 0.0 all-reduce.10.cloned.1.call-update
  282.6 1.6 constant_dynamic-slice_fusion
  284.2 1.3 copy.21
  285.5 31.3 %all-reduce.10.cloned.1.call-done = (f32[256,256]{1,0:T(8,128)}, f32[256,256]{1,0:T(8,128)}, f32[256,256]{1,0:T(8,128)}) async-done(((f32[256,256]{1,0:T(8,128)}, f32[256,256]{1,0:T(8,128)}, f32[256,256]{1,0:T(8,128)}), (f32[256,256]{1,0:T(8,128)}, f32[256,256]{1,0:T(8,128)}, f32[256,256]{1,0:T(8,128)})) %all-reduce.10.cloned.1.call-update) | async-done | bytes 786448 | tf_op jit(solution)/shard_map/psum | solution.py:25
  316.8 1.7 fusion.20
  318.5 1.6 fusion.19
  320.1 0.0 copy-start.6
  320.2 1.8 fusion.33
  322.0 0.6 fusion.34
  322.7 0.4 fusion.14
  323.1 0.6 fusion.18
  323.7 0.0 copy-start.17
  323.7 0.0 copy-start.16
  323.7 0.4 fusion.35
  324.1 0.4 fusion.39
  324.6 0.0 copy-start.15
  324.6 0.6 fusion.13
  325.2 0.0 copy-done.20
  325.2 0.6 fusion.16
  325.8 0.6 fusion.15
  326.4 0.6 fusion.11
  327.0 0.6 fusion.41
  327.6 0.0 copy-done.15
  327.6 1.3 fusion.42
  328.9 0.8 copy.20
  (31 shorter events, 0.1 us)
Async XLA Ops:
  7.2 87.1 %copy-start = (f32[512,1024]{1,0:T(8,128)S(1)}, f32[512,1024]{1,0:T(8,128)}, u32[]{:S(2)}) copy-start(f32[512,1024]{1,0:T(8,128)} %param.15) | copy-start | bytes 6291460
  7.2 46.0 %all-gather.3.cloned.1.call-start = ((), (), s32[]{:S(2)}) async-start(), calls=%async_computation | async-start | bytes 1179648 | tf_op jit(solution)/shard_map/all_gather | solution.py:57
  7.9 86.4 %all-gather.5.cloned.1.call-start = ((), (), s32[]{:S(2)}) async-start(), calls=%async_computation.1 | async-start | bytes 1179648 | tf_op jit(solution)/shard_map/all_gather | solution.py:58
  8.7 126.9 %all-reduce.6.cloned.1.call-start = ((), (), s32[]{:S(2)}) async-start(), calls=%async_computation.2 | async-start | bytes 2097152 | tf_op jit(solution)/shard_map/psum | solution.py:64
  17.6 82.8 %copy-start.22 = (f32[512,64]{0,1:T(8,128)S(1)}, f32[512,64]{0,1:T(8,128)}, u32[]{:S(2)}) copy-start(f32[512,64]{0,1:T(8,128)} %param.16) | copy-start | bytes 393220
  100.4 168.4 %all-reduce.8.cloned.1.call-start = ((), (), s32[]{:S(2)}) async-start(), calls=%async_computation.3 | async-start | bytes 5767168 | tf_op jit(solution)/shard_map/psum | solution.py:68
  113.2 28.0 %copy-start.7 = (f32[256,256]{1,0:T(8,128)S(1)}, f32[256,256]{1,0:T(8,128)}, u32[]{:S(2)}) copy-start(f32[256,256]{1,0:T(8,128)} %param.20) | copy-start | bytes 786436
  135.5 5.7 %copy-start.14 = (f32[512,512]{0,1:T(8,128)S(1)}, f32[512,512]{0,1:T(8,128)}, u32[]{:S(2)}) copy-start(f32[512,512]{0,1:T(8,128)} %all-reduce.6.cloned.1.call-done) | copy-start | bytes 3145732
  137.7 4.2 %copy-start.5 = (f32[256,256]{1,0:T(8,128)S(1)}, f32[256,256]{1,0:T(8,128)}, u32[]{:S(2)}) copy-start(f32[256,256]{1,0:T(8,128)} %param.29) | copy-start | bytes 786436
  142.9 0.8 copy-start.3
  143.7 125.1 %copy-start.12 = (f32[256,256]{1,0:T(8,128)S(1)}, f32[256,256]{1,0:T(8,128)}, u32[]{:S(2)}) copy-start(f32[256,256]{1,0:T(8,128)} %param.24) | copy-start | bytes 786436
  145.4 126.6 %copy-start.9 = (f32[256,256]{1,0:T(8,128)S(1)}, f32[256,256]{1,0:T(8,128)}, u32[]{:S(2)}) copy-start(f32[256,256]{1,0:T(8,128)} %param.18) | copy-start | bytes 786436
  145.4 171.4 %all-reduce.10.cloned.1.call-start = ((), (), s32[]{:S(2)}) async-start(), calls=%async_computation.4 | async-start | bytes 1572864 | tf_op jit(solution)/shard_map/psum | solution.py:25
  268.8 3.2 copy-start.11
  272.0 1.1 copy-start.4
  272.0 3.0 copy-start.2
  273.2 4.4 %copy-start.1 = (f32[256,1024]{1,0:T(8,128)S(1)}, f32[256,1024]{1,0:T(8,128)}, u32[]{:S(2)}) copy-start(f32[256,1024]{1,0:T(8,128)} %all-gather.5.cloned.1.call-done) | copy-start | bytes 3145732
  285.5 36.5 %copy-start.13 = (f32[256,256]{1,0:T(8,128)S(1)}, f32[256,256]{1,0:T(8,128)}, u32[]{:S(2)}) copy-start(f32[256,256]{1,0:T(8,128)} %param.25) | copy-start | bytes 786436
  285.5 37.1 %copy-start.8 = (f32[256,256]{1,0:T(8,128)S(1)}, f32[256,256]{1,0:T(8,128)}, u32[]{:S(2)}) copy-start(f32[256,256]{1,0:T(8,128)} %param.20) | copy-start | bytes 786436
  316.8 5.8 %copy-start.21 = (f32[256,256]{1,0:T(8,128)S(1)}, f32[256,256]{1,0:T(8,128)}, u32[]{:S(2)}) copy-start(f32[256,256]{1,0:T(8,128)} %get-tuple-element.16) | copy-start | bytes 786436
  316.8 6.3 %copy-start.10 = (f32[256,256]{1,0:T(8,128)S(1)}, f32[256,256]{1,0:T(8,128)}, u32[]{:S(2)}) copy-start(f32[256,256]{1,0:T(8,128)} %param.18) | copy-start | bytes 786436
  316.8 6.3 %copy-start.19 = (f32[256,256]{0,1:T(8,128)S(1)}, f32[256,256]{0,1:T(8,128)}, u32[]{:S(2)}) copy-start(f32[256,256]{0,1:T(8,128)} %get-tuple-element.11) | copy-start | bytes 786436
  320.1 4.0 %copy-start.6 = (f32[256,256]{1,0:T(8,128)S(1)}, f32[256,256]{1,0:T(8,128)}, u32[]{:S(2)}) copy-start(f32[256,256]{1,0:T(8,128)} %param.29) | copy-start | bytes 786436
  322.0 2.5 copy-start.18
  323.1 2.1 copy-start.20
  323.7 2.1 copy-start.17
  323.7 2.7 copy-start.16
  324.6 3.1 copy-start.15
Sparse Core Ops, SparseCore 0:
  10.1 42.9 all-gather.2
  55.3 38.9 all-gather.4
  100.5 34.9 all-reduce.5
  145.6 123.1 all-reduce.7
  282.7 34.0 all-reduce.9
where the time goes:
time: 337 us; the launch traced here: 336 us
  waiting for transfers between devices  255 us (76%)
  matrix products  45.5 us (14%)
  blocking collectives  16.7 us (5%)
  between operations  14.2 us (4%)
  local copies, waits for them, and re-layouts  4.61 us (1%)
    psum x1, waiting for transfers between devices, body(): upper_adj = lax.psum(-trans_times(lower_stack, trail_adjoint), 'row')  123 us
    all_gather x1, waiting for transfers between devices, body(): lax.all_gather(upper_old, 'row', axis=0, tiled=True)  41.1 us
    all_gather x1, waiting for transfers between devices, body(): lax.all_gather(upper_new, 'row', axis=0, tiled=True)  35.6 us
    psum x1, waiting for transfers between devices, upper_inner(): summed = lax.psum(terms, 'col')  31.3 us
    dot_general x14, matrix products, times_trans(): lax.dot_general(left, right, (((1,), (1,)), ((), ())), precision=precise)  23 us
    dot_general x14, matrix products, trans_times(): lax.dot_general(left, right, (((0,), (0,)), ((), ())), precision=precise)  22.5 us
    psum x1, waiting for transfers between devices, body(): lower_adj = lax.psum(-times_trans(trail_adjoint, upper_stack), 'col')  22.4 us
    all_gather x1, blocking collectives, body(): lax.all_gather(lower_old, 'col', axis=1, tiled=True)  8.86 us
  transfers between devices with their start and end apart: 5, of which 5 were waited for; matrix products, arithmetic and copies ran while one was open for 2% of the time, Pallas kernels for 0%

commit v1 on v0

--- a/solution.py
+++ b/solution.py
@@ -53,8 +53,11 @@
         lax.all_gather(lower_new, "col", axis=1, tiled=True),
         lax.all_gather(lower_old, "col", axis=1, tiled=True),
     )
+    push_signs_all = lambda vector, axis_no: jnp.concatenate(
+        jax.lax.all_to_all(jnp.stack([vector] * jax.lax.axis_size("row")), "row", 0, 0), axis_no
+    )
     upper_full_new, upper_full_old = (
-        lax.all_gather(upper_new, "row", axis=0, tiled=True),
+        push_signs_all(upper_new, 0),
         lax.all_gather(upper_old, "row", axis=0, tiled=True),
     )
     lower_stack = jnp.concatenate((lower_full_new, lower_full_old), axis=1)

time: 337 us -> 302 us (0.90)
  waiting for transfers between devices: 255 us -> 210 us
  starting transfers between devices: 0.42 us -> 7.69 us
    all_gather x1 -> x0, waiting for transfers between devices: 35.6 us -> none  [body(): lax.all_gather(upper_new, 'row', axis=0, tiled=True)]
    all_to_all x0 -> x1, starting transfers between devices: none -> 7.31 us  [body(): jax.lax.all_to_all(jnp.stack([vector] * jax.lax.axis_size('row')), 'row',...]
    all_gather x1, waiting for transfers between devices: 41.1 us -> 34 us  [body(): lax.all_gather(upper_old, 'row', axis=0, tiled=True)]
  transfers between devices with their start and end apart: 5 -> 5, of which waited for: 5 -> 4; matrix products, arithmetic and copies ran while one was open for 2% -> 4% of each run, Pallas kernels for 0% -> 0%
where the time goes in v1:
time: 302 us
  waiting for transfers between devices  210 us (70%)
  matrix products  47.4 us (16%)
  blocking collectives  15.3 us (5%)
  between operations  14.2 us (5%)
  starting transfers between devices  7.69 us (3%)
  local copies, waits for them, and re-layouts  7.41 us (2%)
    psum x1, waiting for transfers between devices, body(): upper_adj = lax.psum(-trans_times(lower_stack, trail_adjoint), 'row')  123 us
    all_gather x1, waiting for transfers between devices, body(): lax.all_gather(upper_old, 'row', axis=0, tiled=True)  34 us
    psum x1, waiting for transfers between devices, upper_inner(): summed = lax.psum(terms, 'col')  31.3 us
    dot_general x14, matrix products, trans_times(): lax.dot_general(left, right, (((0,), (0,)), ((), ())), precision=precise)  24.6 us
    dot_general x14, matrix products, times_trans(): lax.dot_general(left, right, (((1,), (1,)), ((), ())), precision=precise)  22.7 us
    psum x1, waiting for transfers between devices, body(): lower_adj = lax.psum(-times_trans(trail_adjoint, upper_stack), 'col')  20.7 us
    all_gather x1, blocking collectives, body(): lax.all_gather(lower_new, 'col', axis=1, tiled=True)  7.72 us
    all_gather x1, blocking collectives, body(): lax.all_gather(lower_old, 'col', axis=1, tiled=True)  7.62 us
  transfers between devices with their start and end apart: 5, of which 4 were waited for; matrix products, arithmetic and copies ran while one was open for 4% of the time, Pallas kernels for 0%

profile of v1, /device:TPU:0, one launch (start us, length us, event | category | flops | bytes accessed | tf_op | source)
XLA Modules:
  0.0 301.6 jit_solution(4202098936386270104)
XLA Ops:
  7.2 0.0 copy-start
  7.2 0.0 copy-start.24
  7.2 0.0 all-gather.2.cloned.1.call-start
  7.2 0.7 all-gather.2.cloned.1.call-update
  7.9 2.0 stack.2
  9.9 7.3 %all-to-all-start = ((f32[8,32,1024]{2,1,0:T(8,128)}), f32[8,32,1024]{2,1,0:T(8,128)S(1)}, u32[]{:S(2)}, u32[]{:S(2)}) async-start(f32[8,32,1024]{2,1,0:T(8,128)} %stack.2), calls=%async_computation | async-start | bytes 2097152 | tf_op jit(solution)/shard_map/all_to_all | solution.py:57
  17.2 0.0 all-reduce.6.cloned.1.call-start
  17.3 7.6 %all_gather.10 = f32[512,256]{0,1:T(8,128)} all-gather(f32[512,64]{0,1:T(8,128)S(1)} %copy-done.24), channel_id=1, replica_groups=mesh['row'=8,'col'=4] {'col'}, dimensions={1}, use_global_device_ids=true | all-gather | bytes 655360 | tf_op jit(solution)/shard_map/all_gather | solution.py:54
  24.9 34.0 %all-gather.2.cloned.1.call-done = f32[256,1024]{1,0:T(8,128)} async-done(((f32[32,1024]{1,0:T(8,128)}), f32[256,1024]{1,0:T(8,128)}) %all-gather.2.cloned.1.call-update) | async-done | bytes 1048592 | tf_op jit(solution)/shard_map/all_gather | solution.py:61
  58.9 0.0 all-to-all-done
  58.9 5.8 %fusion.7 = f32[512,512]{0,1:T(8,128)} fusion(f32[512,1024]{1,0:T(8,128)S(1)} %copy-done, f32[256,1024]{1,0:T(8,128)} %all-gather.2.cloned.1.call-done, f32[256,1024]{1,0:T(8,128)S(1)} %bitcast.85), kind=kOutput, calls=%fused_computation.6 | convolution fusion | flops 3222011904 | bytes 5242880 | tf_op jit(solution)/shard_map/dot_general | solution.py:10
  64.7 0.0 all-reduce.6.cloned.1.call-update
  64.7 0.0 all-reduce.8.cloned.1.call-start
  64.7 7.7 %all_gather.9 = f32[512,256]{0,1:T(8,128)S(1)} all-gather(f32[512,64]{0,1:T(8,128)S(1)} %copy-done.25), channel_id=1, replica_groups=mesh['row'=8,'col'=4] {'col'}, dimensions={1}, use_global_device_ids=true | all-gather | bytes 655360 | tf_op jit(solution)/shard_map/all_gather | solution.py:53
  72.5 0.8 copy-done.3
  73.3 6.0 %convolution_negate_fusion = f32[512,1024]{1,0:T(8,128)} fusion(f32[512,1024]{1,0:T(8,128)S(1)} %copy-done, f32[512,256]{0,1:T(8,128)} %all_gather.10, f32[512,256]{0,1:T(8,128)S(1)} %all_gather.9), kind=kOutput, calls=%fused_computation.4 | convolution fusion | flops 3222011904 | bytes 5242880 | tf_op jit(solution)/shard_map/dot_general | solution.py:14
  79.2 20.7 %all-reduce.6.cloned.1.call-done = f32[512,512]{0,1:T(8,128)} async-done(((f32[512,512]{0,1:T(8,128)}), f32[512,512]{0,1:T(8,128)}) %all-reduce.6.cloned.1.call-update) | async-done | bytes 1048592 | tf_op jit(solution)/shard_map/psum | solution.py:67
  99.9 2.2 fusion.26
  102.1 0.0 copy-start.7
  102.1 2.8 convolution_bitcast_fusion.4
  105.0 1.7 convolution_bitcast_fusion.6
  106.7 0.6 convolution_subtract_fusion
  107.3 0.0 copy-done.7
  107.4 1.0 fusion.40
  108.4 0.0 copy-start.5
  108.4 0.8 copy-done.5
  109.2 0.0 copy-done.2
  109.2 1.7 convolution_bitcast_fusion.1
  110.9 0.0 all-reduce.8.cloned.1.call-update
  110.9 0.3 all-reduce.10.cloned.1.call-start
  111.2 122.9 %all-reduce.8.cloned.1.call-done = (f32[512,1024]{1,0:T(8,128)}, f32[256,256]{0,1:T(8,128)}, f32[256,256]{0,1:T(8,128)}, f32[256,256]{0,1:T(8,128)}) async-done(((f32[512,1024]{1,0:T(8,128)}, f32[256,256]{0,1:T(8,128)}, f32[256,256]{0,1:T(8,128)}, f32[256,256]{0,1:T(8,128)}), (f32[512,1024]{1,0:T(8,128)}, f32[256,256]{0,1:T(8,128)}, f32[256,256]{0,1:T(8,128)}, ...) | async-done | bytes 2883600 | tf_op jit(solution)/shard_map/psum | solution.py:71
  234.1 3.2 %fusion.21 = f32[1024,256]{1,0:T(8,128)S(1)} fusion(f32[256,256]{1,0:T(8,128)S(1)} %copy-done.14, f32[512,1024]{1,0:T(8,128)} %get-tuple-element.10), kind=kOutput, calls=%fused_computation.31 | convolution fusion | flops 805306368 | bytes 2359296 | tf_op jit(solution)/shard_map/dot_general | solution.py:14
  237.3 2.5 fusion.32
  239.9 0.0 copy-done.13
  239.9 1.1 fusion.10
  241.0 1.8 fusion.36
  242.8 0.0 copy-done.1
  242.8 2.5 fusion.38
  245.3 2.5 fusion.37
  247.9 0.0 all-reduce.10.cloned.1.call-update
  247.9 1.6 constant_dynamic-slice_fusion
  249.5 1.3 copy.21
  250.8 31.3 %all-reduce.10.cloned.1.call-done = (f32[256,256]{1,0:T(8,128)}, f32[256,256]{1,0:T(8,128)}, f32[256,256]{1,0:T(8,128)}) async-done(((f32[256,256]{1,0:T(8,128)}, f32[256,256]{1,0:T(8,128)}, f32[256,256]{1,0:T(8,128)}), (f32[256,256]{1,0:T(8,128)}, f32[256,256]{1,0:T(8,128)}, f32[256,256]{1,0:T(8,128)})) %all-reduce.10.cloned.1.call-update) | async-done | bytes 786448 | tf_op jit(solution)/shard_map/psum | solution.py:25
  282.1 1.7 fusion.20
  283.8 1.6 fusion.19
  285.4 0.0 copy-start.8
  285.4 1.9 fusion.33
  287.3 0.6 fusion.34
  287.9 0.4 fusion.14
  288.4 0.6 fusion.18
  289.0 0.0 copy-start.19
  289.0 0.0 copy-start.18
  289.0 0.4 fusion.35
  289.4 0.4 fusion.39
  289.8 0.0 copy-start.17
  289.9 0.6 fusion.13
  290.5 0.0 copy-done.22
  290.5 0.6 fusion.16
  291.1 0.6 fusion.15
  291.7 0.6 fusion.11
  292.3 0.6 fusion.41
  292.9 0.0 copy-done.17
  292.9 1.3 fusion.42
  294.2 0.8 copy.20
  (37 shorter events, 0.1 us)
Async XLA Ops:
  7.2 51.7 %copy-start = (f32[512,1024]{1,0:T(8,128)S(1)}, f32[512,1024]{1,0:T(8,128)}, u32[]{:S(2)}) copy-start(f32[512,1024]{1,0:T(8,128)} %param.15) | copy-start | bytes 6291460
  7.2 10.1 %copy-start.24 = (f32[512,64]{0,1:T(8,128)S(1)}, f32[512,64]{0,1:T(8,128)}, u32[]{:S(2)}) copy-start(f32[512,64]{0,1:T(8,128)} %param.19) | copy-start | bytes 393220
  7.2 51.7 %all-gather.2.cloned.1.call-start = ((), (), s32[]{:S(2)}) async-start(), calls=%async_computation.1 | async-start | bytes 1179648 | tf_op jit(solution)/shard_map/all_gather | solution.py:61
  9.9 49.0 %all-to-all-start = ((f32[8,32,1024]{2,1,0:T(8,128)}), f32[8,32,1024]{2,1,0:T(8,128)S(1)}, u32[]{:S(2)}, u32[]{:S(2)}) async-start(f32[8,32,1024]{2,1,0:T(8,128)} %stack.2), calls=%async_computation | async-start | bytes 2097152 | tf_op jit(solution)/shard_map/all_to_all | solution.py:57
  17.2 82.7 %all-reduce.6.cloned.1.call-start = ((), (), s32[]{:S(2)}) async-start(), calls=%async_computation.2 | async-start | bytes 2097152 | tf_op jit(solution)/shard_map/psum | solution.py:67
  58.9 5.8 %copy-start.25 = (f32[512,64]{0,1:T(8,128)S(1)}, f32[512,64]{0,1:T(8,128)}, u32[]{:S(2)}) copy-start(f32[512,64]{0,1:T(8,128)} %param.16) | copy-start | bytes 393220
  64.7 169.4 %all-reduce.8.cloned.1.call-start = ((), (), s32[]{:S(2)}) async-start(), calls=%async_computation.3 | async-start | bytes 5767168 | tf_op jit(solution)/shard_map/psum | solution.py:71
  72.5 0.8 copy-start.3
  79.2 27.5 %copy-start.9 = (f32[256,256]{1,0:T(8,128)S(1)}, f32[256,256]{1,0:T(8,128)}, u32[]{:S(2)}) copy-start(f32[256,256]{1,0:T(8,128)} %param.20) | copy-start | bytes 786436
  99.9 5.1 %copy-start.4 = (f32[512,256]{0,1:T(8,128)S(1)}, f32[512,256]{0,1:T(8,128)}, u32[]{:S(2)}) copy-start(f32[512,256]{0,1:T(8,128)} %copy-done.3) | copy-start | bytes 1572868
  99.9 6.8 %copy-start.16 = (f32[512,512]{0,1:T(8,128)S(1)}, f32[512,512]{0,1:T(8,128)}, u32[]{:S(2)}) copy-start(f32[512,512]{0,1:T(8,128)} %all-reduce.6.cloned.1.call-done) | copy-start | bytes 3145732
  102.1 5.2 %copy-start.7 = (f32[256,256]{1,0:T(8,128)S(1)}, f32[256,256]{1,0:T(8,128)}, u32[]{:S(2)}) copy-start(f32[256,256]{1,0:T(8,128)} %param.29) | copy-start | bytes 786436
  105.0 4.2 %copy-start.2 = (f32[512,256]{0,1:T(8,128)S(1)}, f32[512,256]{0,1:T(8,128)}, u32[]{:S(2)}) copy-start(f32[512,256]{0,1:T(8,128)} %all_gather.10) | copy-start | bytes 1572868
  108.4 0.8 copy-start.5
  109.2 125.0 %copy-start.14 = (f32[256,256]{1,0:T(8,128)S(1)}, f32[256,256]{1,0:T(8,128)}, u32[]{:S(2)}) copy-start(f32[256,256]{1,0:T(8,128)} %param.24) | copy-start | bytes 786436
  110.9 171.2 %all-reduce.10.cloned.1.call-start = ((), (), s32[]{:S(2)}) async-start(), calls=%async_computation.4 | async-start | bytes 1572864 | tf_op jit(solution)/shard_map/psum | solution.py:25
  234.1 5.7 %copy-start.11 = (f32[256,256]{1,0:T(8,128)S(1)}, f32[256,256]{1,0:T(8,128)}, u32[]{:S(2)}) copy-start(f32[256,256]{1,0:T(8,128)} %param.18) | copy-start | bytes 786436
  234.1 5.7 %copy-start.13 = (f32[512,1024]{1,0:T(8,128)S(1)}, f32[512,1024]{1,0:T(8,128)}, u32[]{:S(2)}) copy-start(f32[512,1024]{1,0:T(8,128)} %get-tuple-element.10) | copy-start | bytes 6291460
  239.9 1.1 copy-start.6
  239.9 2.9 copy-start.1
  250.8 36.5 %copy-start.15 = (f32[256,256]{1,0:T(8,128)S(1)}, f32[256,256]{1,0:T(8,128)}, u32[]{:S(2)}) copy-start(f32[256,256]{1,0:T(8,128)} %param.25) | copy-start | bytes 786436
  250.8 37.1 %copy-start.10 = (f32[256,256]{1,0:T(8,128)S(1)}, f32[256,256]{1,0:T(8,128)}, u32[]{:S(2)}) copy-start(f32[256,256]{1,0:T(8,128)} %param.20) | copy-start | bytes 786436
  282.1 5.8 %copy-start.23 = (f32[256,256]{1,0:T(8,128)S(1)}, f32[256,256]{1,0:T(8,128)}, u32[]{:S(2)}) copy-start(f32[256,256]{1,0:T(8,128)} %get-tuple-element.16) | copy-start | bytes 786436
  282.1 6.3 %copy-start.12 = (f32[256,256]{1,0:T(8,128)S(1)}, f32[256,256]{1,0:T(8,128)}, u32[]{:S(2)}) copy-start(f32[256,256]{1,0:T(8,128)} %param.18) | copy-start | bytes 786436
  282.1 6.3 %copy-start.21 = (f32[256,256]{0,1:T(8,128)S(1)}, f32[256,256]{0,1:T(8,128)}, u32[]{:S(2)}) copy-start(f32[256,256]{0,1:T(8,128)} %get-tuple-element.11) | copy-start | bytes 786436
  285.4 4.0 %copy-start.8 = (f32[256,256]{1,0:T(8,128)S(1)}, f32[256,256]{1,0:T(8,128)}, u32[]{:S(2)}) copy-start(f32[256,256]{1,0:T(8,128)} %param.29) | copy-start | bytes 786436
  287.3 2.5 copy-start.20
  288.4 2.1 copy-start.22
  289.0 2.1 copy-start.19
  289.0 2.7 copy-start.18
  289.8 3.1 %copy-start.17 = (f32[256,256]{1,0:T(8,128)}, f32[256,256]{1,0:T(8,128)S(1)}, u32[]{:S(2)}) copy-start(f32[256,256]{1,0:T(8,128)S(1)} %fusion.39) | copy-start | bytes 786436
Sparse Core Ops, SparseCore 0:
  10.1 48.7 all-gather.1
  64.8 35.0 all-reduce.5
  111.0 123.0 all-reduce.7
  248.0 34.0 all-reduce.9
